TPU v7x, 32 devices: a whole 2x2x4 slice. The times are simulated.
32 devices in a mesh: ctx: 16 (over z, y, core), ch: 2 (over x).
Axes of the slice: x: 2, y: 2, z: 4, core: 2. Of those that a mesh axis runs over, the one named last changes fastest.
Arguments:
- tokens: bfloat16 [4096, 4096], P('ctx', 'ch'), may hold values from -6 to 6
- w_in: bfloat16 [4096, 3, 4096], P('ctx', None, 'ch'), may hold values from -0.09375 to 0.09375
- taps: float32 [3, 3, 4096], P(None, None, 'ch'), may hold values from -2 to 2
- modes_gain: float32 [16, 4096], P(None, 'ch'), may hold values from -1.5 to 1.5
- decay: float32 [16, 4096], P(None, 'ch'), may hold values from 0.3 to 300
- skip: float32 [4096], P('ch'), may hold values from -4 to 4
Outputs:
- mixed: bfloat16 [4096, 4096], P('ctx', 'ch')
All inputs are finite; a program needn't handle non-finite values.
Results may differ from a plain program's by a relative error of at most 0.0075.
Values may be sent and summed in bfloat16 or wider, within the bound.
A program may use at most 128 MiB of HBM per device.

v0:
```python
import jax
import jax.numpy as jnp
from jax import lax
from jax.sharding import PartitionSpec as P

highest = lax.Precision.HIGHEST


def from_behind(block, axis, distance):
    devices = range(lax.axis_size(axis))
    route = [(i - distance, i) for i in devices if i - distance in devices]
    return lax.ppermute(block, axis, route)


def carried_in(array, axis, combine, identity):
    devices, here = (lax.axis_size(axis), lax.axis_index(axis))
    everything = jax.tree.map(lambda part: lax.all_gather(part, axis), array)
    start = jax.tree.map(
        lambda part, zero: jnp.broadcast_to(jnp.asarray(zero, part.dtype), part.shape),
        array,
        identity,
    )

    def hop(k, before):
        reached = k < here
        new = combine(before, jax.tree.map(lambda part: part[k], everything))
        return jax.tree.map(lambda a, b: jnp.where(reached, a, b), new, before)

    return lax.fori_loop(0, devices, hop, start)


def chain_states(earlier, later):
    return (earlier[0] * later[0], earlier[1] * later[0] + later[1])


def modal_convolve(signal, rate, weight):
    length, width = signal.shape
    count = length // 32
    blocks = signal.reshape(count, 32, width)
    offsets = jnp.arange(32, dtype=jnp.int32)
    lag_values = offsets.astype(jnp.float32)
    lag_decay = jnp.exp(-rate[None] * lag_values[:, None, None])
    filt_lag = jnp.sum(weight[None] * lag_decay, 1)
    distance = offsets[:, None] - offsets[None, :]
    kernel = jnp.where((distance >= 0)[:, :, None], filt_lag[jnp.clip(distance, 0, 31)], 0.0)
    inside = jnp.einsum(
        "tsc,nsc->ntc", kernel, blocks, precision=highest, preferred_element_type=jnp.float32
    )
    to_end = lag_decay[::-1]
    block_states = jnp.einsum(
        "nsc,smc->nmc", blocks, to_end, precision=highest, preferred_element_type=jnp.float32
    )
    block_factor = jnp.broadcast_to(jnp.exp(-32.0 * rate)[None], block_states.shape)
    running = lax.associative_scan(chain_states, (block_factor, block_states), axis=0)[1]
    local_in = jnp.concatenate([jnp.zeros_like(running[:1]), running[:-1]], 0)
    block_start = (32 * jnp.arange(count, dtype=jnp.int32)).astype(jnp.float32)
    carried_decay = jnp.exp(-rate[None] * block_start[:, None, None])
    growth = jnp.exp(-rate[None] * (lag_values + 1.0)[:, None, None]) * weight[None]

    def finish(incoming):
        entering = local_in + incoming[None] * carried_decay
        carried = jnp.einsum(
            "nmc,tmc->ntc", entering, growth, precision=highest, preferred_element_type=jnp.float32
        )
        return (inside + carried).reshape(length, width)

    device_factor = jnp.exp(-float(length) * rate)
    return (finish, device_factor, running[-1])


def body(tokens, w_in, taps, modes_gain, decay, skip):
    rows = tokens.shape[0]
    channels = w_in.shape[2]
    parts = lax.axis_size("ctx")
    length = rows * parts
    whole = lax.all_gather(tokens, "ch", axis=1, tiled=True)
    piece = lax.all_gather(w_in, "ctx", axis=0, tiled=True)
    flat = piece.reshape(piece.shape[0], 3 * channels)
    projected = jnp.dot(whole, flat, preferred_element_type=jnp.float32)
    projected = projected.astype(jnp.bfloat16).reshape(rows, 3, channels)
    before = from_behind(projected[rows - 2 :], "ctx", 1)
    extended = jnp.concatenate([before, projected], 0).astype(jnp.float32)
    features = taps[0] * extended[2:] + taps[1] * extended[1:-1] + taps[2] * extended[:-2]
    gate_out = features[:, 0]
    product = features[:, 1] * features[:, 2]
    rate = decay / length
    weight = modes_gain * jnp.sqrt(2.0 * rate)
    finish, device_factor, device_state = modal_convolve(product, rate, weight)
    identity = (jnp.ones_like(device_factor), jnp.zeros_like(device_state))
    earlier_states = carried_in((device_factor, device_state), "ctx", chain_states, identity)
    conv = finish(earlier_states[1])
    return (gate_out * (conv + skip * product)).astype(jnp.bfloat16)


def solution(mesh):
    in_specs = (
        P("ctx", "ch"),
        P("ctx", None, "ch"),
        P(None, None, "ch"),
        P(None, "ch"),
        P(None, "ch"),
        P("ch"),
    )
    out_specs = P("ctx", "ch")
    return jax.shard_map(body, mesh=mesh, in_specs=in_specs, out_specs=out_specs, check_vma=False)
```

profile of v0, /device:TPU:16, one launch (start us, length us, event | category | flops | bytes accessed | tf_op | source)
XLA Modules:
  0.0 583.0 jit_solution(8385229775016770324)
XLA Ops:
  7.3 4.7 copy.99
  13.6 13.8 %multiply_exponential_fusion = (f32[32,16,2048]{0,1,2:T(8,128)}, f32[32,2048]{0,1:T(8,128)}) fusion(f32[32]{0:T(128)S(1)} %iota_convert_fusion, f32[16,2048]{0,1:T(8,128)S(1)} %copy.104, f32[16,2048]{0,1:T(8,128)S(1)} %copy.103), kind=kLoop, calls=%fused_computation.12 | loop fusion | flops 3080192 | bytes 4718720 | tf_op jit(solution)/shard_map/exp | solution.py:42
  27.4 15.7 %all-gather.6.cloned.1.call-done = bf16[256,4096]{1,0:T(8,128)(2,1)} async-done(((bf16[256,2048]{1,0:T(8,128)(2,1)}), bf16[256,4096]{1,0:T(8,128)(2,1)}) %all-gather.6.cloned.1.call-update) | async-done | bytes 2097168 | tf_op jit(solution)/shard_map/all_gather | solution.py:76
  43.1 255.6 %all-gather.8.cloned.1.call-done = bf16[4096,3,2048]{0,2,1:T(8,128)(2,1)} async-done(((bf16[256,3,2048]{0,2,1:T(8,128)(2,1)}), bf16[4096,3,2048]{0,2,1:T(8,128)(2,1)}) %all-gather.8.cloned.1.call-update) | async-done | bytes 50331664 | tf_op jit(solution)/shard_map/all_gather | solution.py:77
  298.6 20.6 %convolution_convert_fusion = bf16[256,6144]{1,0:T(8,128)(2,1)S(1)} fusion(bf16[256,4096]{1,0:T(8,128)(2,1)} %all-gather.6.cloned.1.call-done, bf16[4096,6144]{0,1:T(8,128)(2,1)} %bitcast.64), kind=kOutput, calls=%fused_computation.18 | convolution fusion | flops 12886474752 | bytes 55574528 | tf_op jit(solution)/shard_map/dot_general | solution.py:79
  321.4 2.3 collective-permute-start
  325.2 25.0 %rev.3 = f32[32,16,2048]{0,1,2:T(8,128)} reverse(f32[32,16,2048]{0,1,2:T(8,128)} %get-tuple-element.143), dimensions={0} | reverse | bytes 8388608 | tf_op jit(solution)/shard_map/rev | solution.py:49
  350.2 3.2 copy.100
  353.4 2.3 copy.101
  355.7 3.3 maximum_convert_fusion
  359.1 6.3 %fusion.12 = f32[256,3,2048]{0,2,1:T(8,128)S(1)} fusion(f32[258,3,2048]{0,2,1:T(8,128)S(1)} %maximum_convert_fusion, f32[3,2048]{1,0:T(4,128)S(1)} %copy-done.14, f32[3,2048]{1,0:T(4,128)S(1)} %copy-done.15, f32[3,2048]{1,0:T(4,128)S(1)} %copy-done.13), kind=kLoop, calls=%fused_computation.20 | loop fusion | flops 7864320 | bytes 25239552 | tf_op jit(solution)/shard_map/add | solution.py:83
  365.4 2.6 copy-done
  371.5 4.7 copy.107
  376.3 31.1 %fusion.27 = f32[2048,16,8]{1,2,0:T(8,128)} fusion(f32[32,16,2048]{0,1,2:T(8,128)} %rev.3, f32[8,32,2048]{1,0,2:T(8,128)} %copy.107), kind=kOutput, calls=%fused_computation.64 | convolution fusion | flops 100663296 | bytes 7340032 | tf_op jit(solution)/shard_map/nsc,smc->nmc/dot_general | solution.py:50
  407.3 5.4 copy.109
  420.1 6.8 %gather_fusion = f32[1024,2048]{1,0:T(8,128)} fusion(f32[32,2048]{1,0:T(8,128)S(1)} %copy.105, s32[1024]{0:T(1024)S(1)} %broadcast_clamp_fusion), kind=kCustom, calls=%fused_computation | custom fusion | bytes 16781312 | tf_op jit(solution)/shard_map/gather | solution.py:45
  426.9 26.4 %copy.106 = f32[32,32,2048]{1,0,2:T(8,128)} copy(f32[32,32,2048]{2,1,0:T(8,128)} %bitcast.56) | data formatting | bytes 16777216 | tf_op jit(solution)/shard_map/gather | solution.py:45
  453.3 2.3 pad.25
  458.1 57.4 %fusion.1 = f32[2048,8,32]{2,1,0:T(8,128)} fusion(f32[8,32,2048]{1,0,2:T(8,128)} %copy.107, f32[32,32,2048]{1,0,2:T(8,128)} %copy.106, pred[32,32]{1,0:T(8,128)(4,1)S(1)} %subtract_compare_fusion), kind=kOutput, calls=%fused_computation.4 | convolution fusion | flops 203423744 | bytes 12583936 | tf_op jit(solution)/shard_map/tsc,nsc->ntc/dot_general | solution.py:46
  515.5 17.6 %while.14 = (s32[]{:T(128)}, f32[16,2048]{1,0:T(8,128)S(1)}, s32[]{:T(128)}, f32[16,16,2048]{2,1,0:T(8,128)}, f32[16,16,2048]{2,1,0:T(8,128)}, /*index=5*/s32[]{:T(128)}, s32[]{:T(128)}) while((s32[]{:T(128)}, f32[16,2048]{1,0:T(8,128)S(1)}, s32[]{:T(128)}, f32[16,16,2048]{2,1,0:T(8,128)}, f32[16,16,2048]{2,1,0:T(8,128)}, ...), condition=%wide.region_2.3_spmd.clone, body=%wide.region_1.2_spmd.clone.sunk | while | flops 131076 | bytes 524397 | solution.py:29
  534.6 5.0 copy.110
  539.5 24.6 %bitcast_add_fusion.1 = f32[8,32,2048]{1,0,2:T(8,128)} fusion(f32[2048,8,32]{2,1,0:T(8,128)} %fusion.1, f32[8,16,2048]{1,0,2:T(8,128)} %copy.110, f32[32]{0:T(128)S(1)} %broadcast_add_fusion, f32[16,2048]{0,1:T(8,128)S(1)} %copy-done.5, f32[16,2048]{0,1:T(8,128)S(1)} %copy-done.3), kind=kOutput, calls=%fused_computation.14 | convolution fusion | flops 103284736 | bytes 5505152 | tf_op jit(solution)/shard_map/nmc,tmc->ntc/dot_general | solution.py:62
  564.2 5.1 copy.111
  571.2 3.9 fusion.17
  (98 shorter events, 41.1 us)
Async XLA Ops:
  6.5 5.5 copy-start.8
  6.5 5.5 copy-start.16
  6.5 36.5 %all-gather.6.cloned.1.call-start = ((), (), s32[]{:S(2)}) async-start(), calls=%async_computation | async-start | bytes 3145728 | tf_op jit(solution)/shard_map/all_gather | solution.py:76
  7.3 291.4 %all-gather.8.cloned.1.call-start = ((), (), s32[]{:S(2)}) async-start(), calls=%async_computation.1 | async-start | bytes 53477376 | tf_op jit(solution)/shard_map/all_gather | solution.py:77
  12.0 503.5 %all-gather.12.cloned.1.call-start = ((), (), s32[]{:S(2)}) async-start(), calls=%async_computation.3 | async-start | bytes 2228224 | tf_op jit(solution)/shard_map/all_gather | solution.py:17
  12.8 14.6 %copy-start.9 = (f32[16,2048]{1,0:T(8,128)}, f32[16,2048]{1,0:T(8,128)S(1)}, u32[]{:S(2)}) copy-start(f32[16,2048]{1,0:T(8,128)S(1)} %get-tuple-element.151) | copy-start | bytes 393220
  12.8 400.0 %copy-start.11 = (f32[16,2048]{1,0:T(8,128)}, f32[16,2048]{1,0:T(8,128)S(1)}, u32[]{:S(2)}) copy-start(f32[16,2048]{1,0:T(8,128)S(1)} %get-tuple-element.153) | copy-start | bytes 393220
  12.8 502.7 %all-gather.10.cloned.1.call-start = ((), (), s32[]{:S(2)}) async-start(), calls=%async_computation.2 | async-start | bytes 2228224 | tf_op jit(solution)/shard_map/all_gather | solution.py:17
  13.2 14.1 %copy-start.2 = (f32[16,2048]{0,1:T(8,128)}, f32[16,2048]{0,1:T(8,128)S(1)}, u32[]{:S(2)}) copy-start(f32[16,2048]{0,1:T(8,128)S(1)} %copy.103) | copy-start | bytes 393220
  13.6 13.8 %copy-start.4 = (f32[16,2048]{0,1:T(8,128)}, f32[16,2048]{0,1:T(8,128)S(1)}, u32[]{:S(2)}) copy-start(f32[16,2048]{0,1:T(8,128)S(1)} %copy.104) | copy-start | bytes 393220
  319.3 5.9 %copy-start.7 = (bf16[256,6144]{1,0:T(8,128)(2,1)}, bf16[256,6144]{1,0:T(8,128)(2,1)S(1)}, u32[]{:S(2)}) copy-start(bf16[256,6144]{1,0:T(8,128)(2,1)S(1)} %convolution_convert_fusion) | copy-start | bytes 9437188
  321.4 32.0 %collective-permute-start = (bf16[2,3,2048]{2,1,0:T(4,128)(2,1)}, bf16[2,3,2048]{2,1,0:T(4,128)(2,1)}, u32[]{:S(2)}, u32[]{:S(2)}) collective-permute-start(bf16[2,3,2048]{2,1,0:T(4,128)(2,1)} %slice.98), channel_id=1, source_target_pairs={{0,2},{2,4},{4,6},{6,8},{8,10},{10,12},{12,14},{14,16},{16,18},{18... | collective-permute-start | bytes 73736 | tf_op jit(solution)/shard_map/ppermute | solution.py:12
  355.7 3.3 copy-start.13
  355.7 3.3 copy-start.14
  355.7 3.3 copy-start.15
  365.4 2.6 copy-start
  407.3 12.4 %copy-start.1 = (f32[32,2048]{0,1:T(8,128)S(1)}, f32[32,2048]{0,1:T(8,128)}, u32[]{:S(2)}) copy-start(f32[32,2048]{0,1:T(8,128)} %get-tuple-element.144) | copy-start | bytes 786436
  426.9 28.8 %copy-start.6 = (f32[4,16,2048]{2,1,0:T(8,128)S(1)}, f32[4,16,2048]{2,1,0:T(8,128)}, u32[]{:S(2)}) copy-start(f32[4,16,2048]{2,1,0:T(8,128)} %pad.23) | copy-start | bytes 1572868
  426.9 28.8 %copy-start.12 = (f32[16,2048]{1,0:T(8,128)S(1)}, f32[16,2048]{1,0:T(8,128)}, u32[]{:S(2)}) copy-start(f32[16,2048]{1,0:T(8,128)} %copy-done.11) | copy-start | bytes 393220
  458.1 75.0 %copy-start.10 = (f32[16,2048]{1,0:T(8,128)S(1)}, f32[16,2048]{1,0:T(8,128)}, u32[]{:S(2)}) copy-start(f32[16,2048]{1,0:T(8,128)} %copy-done.9) | copy-start | bytes 393220
  515.5 24.1 %copy-start.3 = (f32[16,2048]{0,1:T(8,128)S(1)}, f32[16,2048]{0,1:T(8,128)}, u32[]{:S(2)}) copy-start(f32[16,2048]{0,1:T(8,128)} %copy-done.2) | copy-start | bytes 393220
  515.5 24.1 %copy-start.5 = (f32[16,2048]{0,1:T(8,128)S(1)}, f32[16,2048]{0,1:T(8,128)}, u32[]{:S(2)}) copy-start(f32[16,2048]{0,1:T(8,128)} %copy-done.4) | copy-start | bytes 393220
  564.2 7.0 %copy-start.17 = (f32[2048]{0:T(1024)S(1)}, f32[2048]{0:T(1024)}, u32[]{:S(2)}) copy-start(f32[2048]{0:T(1024)} %param.13) | copy-start | bytes 24580
Sparse Core Ops, SparseCore 0:
  8.9 34.1 all-gather.5
  44.6 253.9 all-gather.7
  300.8 39.4 all-gather.11
  419.8 39.6 all-gather.9
where the time goes:
time: 589 us; the launch traced here: 583 us
  waiting for transfers between devices  272 us (46%)
  matrix products  134 us (23%)
  local copies, waits for them, and re-layouts  109 us (19%)
  other arithmetic  51.9 us (9%)
  between operations  13.5 us (2%)
    all_gather x1, waiting for transfers between devices, body(): piece = lax.all_gather(w_in, 'ctx', axis=0, tiled=True)  256 us
    dot_general x1, matrix products, modal_convolve(): jnp.einsum('tsc,nsc->ntc', kernel, blocks, precision=highest, preferred_e...  57.4 us
    gather x2, local copies, waits for them, and re-layouts, modal_convolve(): filt_lag[jnp.clip(distance, 0, 31)]  33.2 us
    dot_general x1, matrix products, modal_convolve(): jnp.einsum('nsc,smc->nmc', blocks, to_end, precision=highest, preferred_e...  31.1 us
    rev x1, local copies, waits for them, and re-layouts, modal_convolve(): to_end = lag_decay[::-1]  25 us
    dot_general x1, matrix products, finish(): jnp.einsum('nmc,tmc->ntc', entering, growth, precision=highest, preferred...  24.6 us
    dot_general x1, matrix products, body(): projected = jnp.dot(whole, flat, preferred_element_type=jnp.float32)  20.6 us
    select_n x16, other arithmetic, hop(): return jax.tree.map(lambda a, b: jnp.where(reached, a, b), new, before)  17.3 us
  transfers between devices with their start and end apart: 5, of which 2 were waited for; matrix products, arithmetic and copies ran while one was open for 40% of the time, Pallas kernels for 0%

commit v1 on v0

v1 whole, which is shorter than its diff:
```python
import functools

import jax
import jax.numpy as jnp
from jax import lax
from jax.experimental import pallas as pl
from jax.experimental.pallas import tpu as pltpu
from jax.sharding import PartitionSpec as P

SEGS = 8
LANES = 128


def flip(index, bits):
    out, bit = index, 1
    while bit <= bits:
        if bits & bit:
            out = out + bit - 2 * bit * ((index // bit) % 2)
        bit *= 2
    return out


def flip_traced(index, bits, count):
    out, bit = index, 1
    while bit < count:
        out = out + ((bits // bit) % 2) * (bit - 2 * bit * ((index // bit) % 2))
        bit *= 2
    return out


def piece_order(i, count):
    quarter = count // 4
    j = jnp.maximum(i - quarter, 0)
    turn = j % 3
    later = 2 * quarter + quarter * turn - 3 * quarter * (turn // 2) + j // 3
    return jnp.where(i < quarter, i, later)


def kernel(
    n_ctx, n_ch, groups,
    tokens, w_send, taps, gains, rates, skip, out,
    tok, w_recv, acc, prod, gate, state, ends, carry, sent, halo, halo_out,
    tok_ssem, tok_rsem, w_ssem, w_rsem, out_ssem, out_rsem, st_ssem, st_rsem, halo_sems, local_sems,
):
    rows, width = tokens.shape
    wide = w_send.shape[2] // 3
    teams = n_ctx // groups
    span = groups * rows
    seg = span // SEGS
    lane_groups = wide // LANES
    ctx, ch = lax.axis_index("ctx"), lax.axis_index("ch")
    team, place = ctx // groups, ctx % groups

    hops = [("ctx", b) for b in reversed([2**i for i in range(1, groups.bit_length() - 1)])]
    hops += [("ch", b) for b in reversed([2**i for i in range(n_ch.bit_length() - 1)])]
    hops += [("ctx", 1)]
    depth = len(hops)

    def target(hop):
        axis, bit = hop
        return (flip(ctx, bit), ch) if axis == "ctx" else (ctx, flip(ch, bit))

    def slot_of(mask):
        cbits = sum(hops[i][1] for i in range(depth) if mask >> i & 1 and hops[i][0] == "ctx")
        hbits = sum(hops[i][1] for i in range(depth) if mask >> i & 1 and hops[i][0] == "ch")
        return flip(ch, hbits) * groups + flip(place, cbits)

    barrier = pltpu.get_barrier_semaphore()

    @pl.loop(1, n_ctx)
    def _(m):
        pl.semaphore_signal(barrier, inc=1, device_id=(flip_traced(ctx, m, n_ctx), ch), device_id_type=pl.DeviceIdType.MESH)

    ch_hops = [hop for hop in hops if hop[0] == "ch"]
    for hop in ch_hops:
        pl.semaphore_signal(barrier, inc=1, device_id=target(hop), device_id_type=pl.DeviceIdType.MESH)
    own_tok = pltpu.make_async_copy(tokens, tok.at[slot_of(0)], local_sems.at[0])
    own_tok.start()
    own_w = pltpu.make_async_copy(w_send.at[place], w_recv.at[0], local_sems.at[1])
    own_w.start()
    pl.semaphore_wait(barrier, n_ctx - 1 + len(ch_hops))

    def tok_copy(mask, i):
        src = tokens if mask == 0 else tok.at[slot_of(mask)]
        return pltpu.make_async_remote_copy(
            src_ref=src,
            dst_ref=tok.at[slot_of(mask)],
            send_sem=tok_ssem.at[mask, i],
            recv_sem=tok_rsem.at[mask | 1 << i],
            device_id=target(hops[i]),
            device_id_type=pl.DeviceIdType.MESH,
        )

    def arrived(mask):
        top = mask.bit_length() - 1
        pltpu.make_async_remote_copy(
            src_ref=tok.at[slot_of(mask)],
            dst_ref=tok.at[slot_of(mask)],
            send_sem=tok_ssem.at[0, top],
            recv_sem=tok_rsem.at[mask],
            device_id=target(hops[top]),
            device_id_type=pl.DeviceIdType.MESH,
        ).wait_recv()

    for i in range(depth):
        tok_copy(0, i).start()

    def w_copy(m):
        peer = flip_traced(ctx, m, n_ctx)
        return pltpu.make_async_remote_copy(
            src_ref=w_send.at[peer % groups],
            dst_ref=w_recv.at[m],
            send_sem=w_ssem.at[m],
            recv_sem=w_rsem.at[m],
            device_id=(peer, ch),
            device_id_type=pl.DeviceIdType.MESH,
        )

    @pl.loop(1, n_ctx)
    def _(i):
        w_copy(piece_order(i, n_ctx)).start()

    acc[...] = jnp.zeros_like(acc)
    masks = sorted(range(1, 2**depth), key=lambda m: (m.bit_length() if m.bit_length() == depth else 0, bin(m).count("1"), m))
    for mask in masks:
        arrived(mask)
        for i in range(mask.bit_length(), depth):
            tok_copy(mask, i).start()
    own_tok.wait()
    own_w.wait()

    tall = 2 if groups % 2 == 0 else 1
    header = SEGS

    @pl.loop(0, n_ctx)
    def _(i):
        m = piece_order(i, n_ctx)

        @pl.when(i > 0)
        def _():
            w_copy(m).wait_recv()

        depth_rows = w_recv.shape[1]
        first = flip_traced(ctx, m, n_ctx) * depth_rows
        half, column = first // width, first % width

        @pl.loop(0, groups // tall)
        def _(part):
            left = tok[pl.ds(half * groups + part * tall, tall), :, pl.ds(pl.multiple_of(column, LANES), depth_rows)]
            left = left.reshape(tall * rows, depth_rows)
            where = pl.ds(pl.multiple_of(header + part * tall * rows, 8), tall * rows)
            acc[where, :] += jnp.dot(left, w_recv[m], preferred_element_type=jnp.float32)

    @pl.loop(0, span // 64)
    def _(part):
        where = pl.ds(pl.multiple_of(header + part * 64, 8), 64)
        acc[where, :] = acc[where, :].astype(jnp.bfloat16).astype(jnp.float32)

    halo_out[...] = acc[span : span + header, :]

    def halo_copy():
        return pltpu.make_async_remote_copy(
            src_ref=halo_out,
            dst_ref=halo,
            send_sem=halo_sems.at[0],
            recv_sem=halo_sems.at[1],
            device_id=((ctx + groups) % n_ctx, ch),
            device_id_type=pl.DeviceIdType.MESH,
        )

    @pl.when(team < teams - 1)
    def _():
        halo_copy().start()

    acc[0:header, :] = jnp.zeros((header, acc.shape[1]), jnp.float32)

    @pl.when(team > 0)
    def _():
        halo_copy().wait_recv()
        acc[0:header, :] = halo[...]

    @pl.loop(0, SEGS)
    def _(s):
        base = pl.multiple_of(s * seg, 8)
        for g in range(lane_groups):
            features = []
            for j in range(3):
                lanes = slice(j * wide + g * LANES, j * wide + (g + 1) * LANES)
                block = acc[pl.ds(base, seg + header), lanes]
                total = taps[0, j : j + 1, g * LANES : (g + 1) * LANES] * block[header:]
                total += taps[1, j : j + 1, g * LANES : (g + 1) * LANES] * pltpu.roll(block, 1, 0)[header:]
                total += taps[2, j : j + 1, g * LANES : (g + 1) * LANES] * pltpu.roll(block, 2, 0)[header:]
                features.append(total)
            gate[g, pl.ds(s, seg, stride=SEGS), :] = features[0]
            prod[g, pl.ds(s, seg, stride=SEGS), :] = features[1] * features[2]

    modes = rates.shape[0]

    def row(ref, m, g):
        return jnp.broadcast_to(ref[m : m + 1, g * LANES : (g + 1) * LANES], (SEGS, LANES))

    for g in range(lane_groups):
        keep = [jnp.exp(-row(rates, m, g)) for m in range(modes)]

        def step(t, states):
            x = prod[g, pl.ds(pl.multiple_of(t * SEGS, SEGS), SEGS), :]
            return tuple(a * s + x for a, s in zip(keep, states))

        zeros = tuple(jnp.zeros((SEGS, LANES), jnp.float32) for _ in range(modes))
        last = lax.fori_loop(0, seg, step, zeros, unroll=2)
        for m in range(modes):
            state[m, :, g * LANES : (g + 1) * LANES] = last[m]

    jump = jnp.exp(-rates[...] * float(seg))
    running = jnp.zeros_like(jump)
    for s in range(SEGS):
        ending = state[:, s, :]
        state[:, s, :] = running
        running = running * jump + ending
    ends[...] = running

    def state_copy(k):
        return pltpu.make_async_remote_copy(
            src_ref=ends,
            dst_ref=carry.at[k],
            send_sem=st_ssem.at[k],
            recv_sem=st_rsem.at[k],
            device_id=((ctx + k * groups) % n_ctx, ch),
            device_id_type=pl.DeviceIdType.MESH,
        )

    carry[0] = jnp.zeros_like(jump)
    for k in range(1, teams):
        @pl.when(team + k < teams)
        def _():
            state_copy(k).start()
    for k in range(1, teams):
        @pl.when(team >= k)
        def _():
            state_copy(k).wait_recv()
            carry[0] += carry[k] * jnp.exp(-rates[...] * float((k - 1) * span))
    incoming = carry[0]
    for s in range(SEGS):
        state[:, s, :] = state[:, s, :] + incoming * jnp.exp(-rates[...] * float(s * seg))

    for g in range(lane_groups):
        keep = [jnp.exp(-row(rates, m, g)) for m in range(modes)]
        weight = [row(gains, m, g) * jnp.sqrt(2.0 * row(rates, m, g)) for m in range(modes)]
        direct = jnp.broadcast_to(skip[0:1, g * LANES : (g + 1) * LANES], (SEGS, LANES))

        def step(t, states):
            where = pl.ds(pl.multiple_of(t * SEGS, SEGS), SEGS)
            x = prod[g, where, :]
            states = tuple(a * s + x for a, s in zip(keep, states))
            terms = [w * s for w, s in zip(weight, states)] + [direct * x]
            while len(terms) > 1:
                terms = [a + b for a, b in zip(terms[::2], terms[1::2])] + ([terms[-1]] if len(terms) % 2 else [])
            gate[g, where, :] = gate[g, where, :] * terms[0]
            return states

        start = tuple(state[m, :, g * LANES : (g + 1) * LANES] for m in range(modes))
        lax.fori_loop(0, seg, step, start)

    @pl.loop(0, SEGS)
    def _(s):
        for g in range(lane_groups):
            value = gate[g, pl.ds(s, seg, stride=SEGS), :]
            sent[pl.ds(pl.multiple_of(s * seg, 8), seg), g * LANES : (g + 1) * LANES] = value.astype(sent.dtype)

    columns = pl.ds(pl.multiple_of(place * wide, LANES), wide)

    def out_rows(p):
        return sent.at[pl.ds(pl.multiple_of(p * rows, 16), rows), :]

    def out_copy(d):
        peer = flip_traced(place, d, groups)
        return pltpu.make_async_remote_copy(
            src_ref=out_rows(peer),
            dst_ref=out.at[:, columns],
            send_sem=out_ssem.at[d],
            recv_sem=out_rsem.at[d],
            device_id=(team * groups + peer, ch),
            device_id_type=pl.DeviceIdType.MESH,
        )

    def out_arrival(d):
        peer = flip_traced(place, d, groups)
        spot = out.at[:, pl.ds(pl.multiple_of(peer * wide, LANES), wide)]
        pltpu.make_async_remote_copy(
            src_ref=spot,
            dst_ref=spot,
            send_sem=out_ssem.at[d],
            recv_sem=out_rsem.at[d],
            device_id=(team * groups + peer, ch),
            device_id_type=pl.DeviceIdType.MESH,
        ).wait_recv()

    own_out = pltpu.make_async_copy(out_rows(place), out.at[:, columns], local_sems.at[2])

    @pl.loop(1, groups)
    def _(d):
        out_copy(groups - d).start()

    own_out.start()
    for i in range(depth):
        tok_copy(0, i).wait_send()
    for mask in masks:
        for i in range(mask.bit_length(), depth):
            tok_copy(mask, i).wait_send()

    @pl.loop(1, n_ctx)
    def _(m):
        w_copy(m).wait_send()

    @pl.when(team < teams - 1)
    def _():
        halo_copy().wait_send()

    for k in range(1, teams):
        @pl.when(team + k < teams)
        def _():
            state_copy(k).wait_send()

    @pl.loop(1, groups)
    def _(d):
        out_arrival(d)
        out_copy(d).wait_send()

    own_out.wait()


def body(n_ctx, n_ch, tokens, w_in, taps, modes_gain, decay, skip):
    rows, width = tokens.shape
    e_rows, _, channels = w_in.shape
    modes = decay.shape[0]
    groups = min(n_ctx // 2, channels // LANES)
    teams = n_ctx // groups
    wide = channels // groups
    span = groups * rows
    depth = (groups * n_ch).bit_length() - 1
    place = lax.axis_index("ctx") % groups

    w_send = w_in.reshape(e_rows, 3, groups, wide).transpose(2, 0, 1, 3).reshape(groups, e_rows, 3 * wide)

    def part(array):
        return lax.dynamic_slice_in_dim(array, place * wide, wide, array.ndim - 1)

    rates = part(decay) / (rows * n_ctx)
    vmem = pl.BlockSpec(memory_space=pltpu.VMEM)
    hbm = pl.BlockSpec(memory_space=pl.ANY)
    dma = pltpu.SemaphoreType.DMA
    f32 = jnp.float32
    return pl.pallas_call(
        functools.partial(kernel, n_ctx, n_ch, groups),
        out_shape=jax.ShapeDtypeStruct((rows, channels), jnp.bfloat16),
        in_specs=[hbm, hbm, vmem, vmem, vmem, vmem],
        out_specs=hbm,
        scratch_shapes=[
            pltpu.VMEM((n_ch * groups, rows, width), tokens.dtype),
            pltpu.VMEM((n_ctx, e_rows, 3 * wide), w_in.dtype),
            pltpu.VMEM((SEGS + span, 3 * wide), f32),
            pltpu.VMEM((wide // LANES, span, LANES), f32),
            pltpu.VMEM((wide // LANES, span, LANES), f32),
            pltpu.VMEM((modes, SEGS, wide), f32),
            pltpu.VMEM((modes, wide), f32),
            pltpu.VMEM((teams, modes, wide), f32),
            pltpu.VMEM((span, wide), jnp.bfloat16),
            pltpu.VMEM((SEGS, 3 * wide), f32),
            pltpu.VMEM((SEGS, 3 * wide), f32),
            dma((2**depth, depth)),
            dma((2**depth,)),
            dma((n_ctx,)),
            dma((n_ctx,)),
            dma((groups,)),
            dma((groups,)),
            dma((teams,)),
            dma((teams,)),
            dma((2,)),
            dma((3,)),
        ],
        compiler_params=pltpu.CompilerParams(
            collective_id=0, has_side_effects=True, vmem_limit_bytes=60 * 1024 * 1024
        ),
    )(tokens, w_send, part(taps), part(modes_gain), rates, part(skip[None]))


def solution(mesh):
    in_specs = (
        P("ctx", "ch"),
        P("ctx", None, "ch"),
        P(None, None, "ch"),
        P(None, "ch"),
        P(None, "ch"),
        P("ch"),
    )
    step = functools.partial(body, mesh.shape["ctx"], mesh.shape["ch"])
    return jax.shard_map(step, mesh=mesh, in_specs=in_specs, out_specs=P("ctx", "ch"), check_vma=False)
```

time: 589 us -> 198 us (0.34); the launches traced: 583 us -> 198 us
  waiting for transfers between devices: 272 us -> 0 us
  Pallas kernels: 0 us -> 183 us
  matrix products: 134 us -> 0 us
  local copies, waits for them, and re-layouts: 109 us -> 13.8 us
  other arithmetic: 51.9 us -> 1.35 us
  between operations: 13.5 us -> 0.02 us
    all_gather x4 -> x0, waiting for transfers between devices: 271 us -> none  [the longest x1 256 us: body(): piece = lax.all_gather(w_in, 'ctx', axis=0, tiled=True)]
    pallas_call x0 -> x1, Pallas kernels: none -> 183 us  [body(): pl.pallas_call(functools.partial(kernel, n_ctx, n_ch, groups), out_shape=...]
    dot_general x4 -> x0, matrix products: 134 us -> none  [the longest x1 57.4 us: modal_convolve(): jnp.einsum('tsc,nsc->ntc', kernel, blocks, precision=highest, preferred_e...]
    gather x2 -> x0, local copies, waits for them, and re-layouts: 33.2 us -> none  [modal_convolve(): filt_lag[jnp.clip(distance, 0, 31)]]
    rev x1 -> x0, local copies, waits for them, and re-layouts: 25 us -> none  [modal_convolve(): to_end = lag_decay[::-1]]
    select_n x17 -> x0, other arithmetic: 17.3 us -> none  [the longest x16 17.3 us: hop(): return jax.tree.map(lambda a, b: jnp.where(reached, a, b), new, before)]
    exp x2 -> x0, other arithmetic: 14.5 us -> none  [the longest x1 13.8 us: modal_convolve(): lag_decay = jnp.exp(-rate[None] * lag_values[:, None, None])]
    add x9 -> x0, other arithmetic: 11.2 us -> none  [the longest x1 6.28 us: body(): taps[0] * extended[2:] + taps[1] * extended[1:-1] + taps[2] * extended[:-2]]
  transfers between devices with their start and end apart: 5 -> 0, of which waited for: 2 -> 0; matrix products, arithmetic and copies ran while one was open for 40% -> 0% of each run, Pallas kernels for 0% -> 0%
where the time goes in v1:
time: 198 us
  Pallas kernels  183 us (92%)
  local copies, waits for them, and re-layouts  13.8 us (7%)
    pallas_call x1, Pallas kernels, body(): pl.pallas_call(functools.partial(kernel, n_ctx, n_ch, groups), out_shape=...  183 us
    unnamed x4, local copies, waits for them, and re-layouts  7.02 us

profile of v1, /device:TPU:16, one launch (start us, length us, event | category | flops | bytes accessed | tf_op | source)
XLA Modules:
  0.0 198.1 jit_solution(12794104535216934428)
XLA Ops:
  0.0 0.0 copy-start
  0.0 4.7 %copy.9 = bf16[256,3,2048]{0,2,1:T(8,128)(2,1)} copy(bf16[256,3,2048]{2,0,1:T(8,128)(2,1)} %param.7) | data formatting | bytes 6291456 | tf_op args[1]
  4.7 2.1 %copy.10 = bf16[8,256,3,256]{1,3,2,0:T(8,128)(2,1)S(1)} copy(bf16[8,256,3,256]{1,3,0,2:T(8,128)(2,1)} %bitcast.6) | data formatting | bytes 6291456 | tf_op jit(solution)/shard_map/transpose | solution.py:343
  6.8 2.8 %copy.11.w_send = bf16[8,256,768]{2,1,0:T(8,128)(2,1)} copy(bf16[8,256,768]{1,2,0:T(8,128)(2,1)S(1)} %bitcast.5) | data formatting | bytes 6291456 | tf_op jit(solution)/shard_map/reshape | solution.py:343
  9.6 0.0 copy-done
  9.6 0.6 constant_dynamic-slice_fusion.1.taps
  10.2 1.4 dynamic-slice_multiply_fusion
  11.6 1.3 dynamic-slice.3
  12.9 182.9 %shard_map.64 = bf16[256,2048]{1,0:T(8,128)(2,1)} custom-call(bf16[256,2048]{1,0:T(8,128)(2,1)} %tokens.1, bf16[8,256,768]{2,1,0:T(8,128)(2,1)} %copy.11.w_send, f32[3,3,256]{2,1,0:T(4,128)} %constant_dynamic-slice_fusion.1.taps, f32[16,256]{1,0:T(8,128)} %get-tuple-element.6.gains, f32[16,256]{1,0:T(8,128)} %get-tuple-element.5.rates, f32[1,256]{1,0:T(1,128)} %bitcast.7), custom_call_target="tpu_custom_call" | custom-call | tf_op jit(solution)/shard_map/pallas_call | solution.py:353
  195.8 2.3 %copy.13 = bf16[256,2048]{1,0:T(8,128)(2,1)} copy(bf16[256,2048]{1,0:T(8,128)(2,1)} %shard_map.64) | data formatting | bytes 2097152
Async XLA Ops:
  0.0 9.6 %copy-start = (f32[3,3,2048]{2,1,0:T(4,128)S(1)}, f32[3,3,2048]{2,1,0:T(4,128)}, u32[]{:S(2)}) copy-start(f32[3,3,2048]{2,1,0:T(4,128)} %param.8) | copy-start | bytes 221188

commit v2 on v1

--- a/solution.py
+++ b/solution.py
@@ -38,12 +38,12 @@
 
 def kernel(
     n_ctx, n_ch, groups,
-    tokens, w_send, taps, gains, rates, skip, out,
-    tok, w_recv, acc, prod, gate, state, ends, carry, sent, halo, halo_out,
+    tokens, w_send, all_taps, all_gains, all_decay, all_skip, out,
+    taps, gains, rates, skip, tok, w_recv, acc, prod, gate, state, ends, carry, sent, halo, halo_out,
     tok_ssem, tok_rsem, w_ssem, w_rsem, out_ssem, out_rsem, st_ssem, st_rsem, halo_sems, local_sems,
 ):
     rows, width = tokens.shape
-    wide = w_send.shape[2] // 3
+    wide = w_send.shape[2] // groups
     teams = n_ctx // groups
     span = groups * rows
     seg = span // SEGS
@@ -76,8 +76,21 @@
         pl.semaphore_signal(barrier, inc=1, device_id=target(hop), device_id_type=pl.DeviceIdType.MESH)
     own_tok = pltpu.make_async_copy(tokens, tok.at[slot_of(0)], local_sems.at[0])
     own_tok.start()
-    own_w = pltpu.make_async_copy(w_send.at[place], w_recv.at[0], local_sems.at[1])
+
+    def w_columns(p):
+        return w_send.at[:, :, pl.ds(pl.multiple_of(p * wide, LANES), wide)]
+
+    own_w = pltpu.make_async_copy(w_columns(place), w_recv.at[0], local_sems.at[1])
     own_w.start()
+    own_lanes = pl.ds(pl.multiple_of(place * wide, LANES), wide)
+    own_small = [
+        pltpu.make_async_copy(all_taps.at[:, :, own_lanes], taps, local_sems.at[3]),
+        pltpu.make_async_copy(all_gains.at[:, own_lanes], gains, local_sems.at[4]),
+        pltpu.make_async_copy(all_decay.at[:, own_lanes], rates, local_sems.at[5]),
+        pltpu.make_async_copy(all_skip.at[:, own_lanes], skip, local_sems.at[6]),
+    ]
+    for copy in own_small:
+        copy.start()
     pl.semaphore_wait(barrier, n_ctx - 1 + len(ch_hops))
 
     def tok_copy(mask, i):
@@ -108,7 +121,7 @@
     def w_copy(m):
         peer = flip_traced(ctx, m, n_ctx)
         return pltpu.make_async_remote_copy(
-            src_ref=w_send.at[peer % groups],
+            src_ref=w_columns(peer % groups),
             dst_ref=w_recv.at[m],
             send_sem=w_ssem.at[m],
             recv_sem=w_rsem.at[m],
@@ -128,6 +141,9 @@
             tok_copy(mask, i).start()
     own_tok.wait()
     own_w.wait()
+    for copy in own_small:
+        copy.wait()
+    rates[...] = rates[...] / (rows * n_ctx)
 
     tall = 2 if groups % 2 == 0 else 1
     header = SEGS
@@ -140,7 +156,7 @@
         def _():
             w_copy(m).wait_recv()
 
-        depth_rows = w_recv.shape[1]
+        depth_rows = w_recv.shape[2]
         first = flip_traced(ctx, m, n_ctx) * depth_rows
         half, column = first // width, first % width
 
@@ -149,7 +165,9 @@
             left = tok[pl.ds(half * groups + part * tall, tall), :, pl.ds(pl.multiple_of(column, LANES), depth_rows)]
             left = left.reshape(tall * rows, depth_rows)
             where = pl.ds(pl.multiple_of(header + part * tall * rows, 8), tall * rows)
-            acc[where, :] += jnp.dot(left, w_recv[m], preferred_element_type=jnp.float32)
+            for j in range(3):
+                lanes = slice(j * wide, (j + 1) * wide)
+                acc[where, lanes] += jnp.dot(left, w_recv[m, j], preferred_element_type=jnp.float32)
 
     @pl.loop(0, span // 64)
     def _(part):
@@ -338,26 +356,22 @@
     wide = channels // groups
     span = groups * rows
     depth = (groups * n_ch).bit_length() - 1
-    place = lax.axis_index("ctx") % groups
-
-    w_send = w_in.reshape(e_rows, 3, groups, wide).transpose(2, 0, 1, 3).reshape(groups, e_rows, 3 * wide)
-
-    def part(array):
-        return lax.dynamic_slice_in_dim(array, place * wide, wide, array.ndim - 1)
-
-    rates = part(decay) / (rows * n_ctx)
-    vmem = pl.BlockSpec(memory_space=pltpu.VMEM)
+    w_send = w_in.transpose(1, 0, 2)
     hbm = pl.BlockSpec(memory_space=pl.ANY)
     dma = pltpu.SemaphoreType.DMA
     f32 = jnp.float32
     return pl.pallas_call(
         functools.partial(kernel, n_ctx, n_ch, groups),
         out_shape=jax.ShapeDtypeStruct((rows, channels), jnp.bfloat16),
-        in_specs=[hbm, hbm, vmem, vmem, vmem, vmem],
+        in_specs=[hbm] * 6,
         out_specs=hbm,
         scratch_shapes=[
+            pltpu.VMEM((3, 3, wide), f32),
+            pltpu.VMEM((modes, wide), f32),
+            pltpu.VMEM((modes, wide), f32),
+            pltpu.VMEM((1, wide), f32),
             pltpu.VMEM((n_ch * groups, rows, width), tokens.dtype),
-            pltpu.VMEM((n_ctx, e_rows, 3 * wide), w_in.dtype),
+            pltpu.VMEM((n_ctx, 3, e_rows, wide), w_in.dtype),
             pltpu.VMEM((SEGS + span, 3 * wide), f32),
             pltpu.VMEM((wide // LANES, span, LANES), f32),
             pltpu.VMEM((wide // LANES, span, LANES), f32),
@@ -376,12 +390,12 @@
             dma((teams,)),
             dma((teams,)),
             dma((2,)),
-            dma((3,)),
+            dma((7,)),
         ],
         compiler_params=pltpu.CompilerParams(
             collective_id=0, has_side_effects=True, vmem_limit_bytes=60 * 1024 * 1024
         ),
-    )(tokens, w_send, part(taps), part(modes_gain), rates, part(skip[None]))
+    )(tokens, w_send, taps, modes_gain, decay, skip[None])
 
 
 def solution(mesh):

time: 198 us -> 184 us (0.929)
  local copies, waits for them, and re-layouts: 13.8 us -> 2.3 us
  Pallas kernels: 183 us -> 181 us
    unnamed x4 -> x1, local copies, waits for them, and re-layouts: 7.02 us -> 2.3 us
    reshape x1 -> x0, local copies, waits for them, and re-layouts: 2.8 us -> none  [body(): w_in.reshape(e_rows, 3, groups, wide).transpose(2, 0, 1, 3)]
    transpose x1 -> x0, local copies, waits for them, and re-layouts: 2.09 us -> none  [body(): w_in.reshape(e_rows, 3, groups, wide).transpose(2, 0, 1, 3)]
where the time goes in v2:
time: 184 us
  Pallas kernels  181 us (98%)
  local copies, waits for them, and re-layouts  2.3 us (1%)
    pallas_call x1, Pallas kernels, body(): pl.pallas_call(functools.partial(kernel, n_ctx, n_ch, groups), out_shape=...  181 us

profile of v2, /device:TPU:16, one launch (start us, length us, event | category | flops | bytes accessed | tf_op | source)
XLA Modules:
  0.0 183.8 jit_solution(1935986758379947856)
XLA Ops:
  0.0 181.5 %shard_map.64 = bf16[256,2048]{1,0:T(8,128)(2,1)} custom-call(bf16[256,2048]{1,0:T(8,128)(2,1)} %tokens.1, bf16[3,256,2048]{2,1,0:T(8,128)(2,1)} %bitcast.2, f32[3,3,2048]{2,1,0:T(4,128)} %all_taps.1, f32[16,2048]{1,0:T(8,128)} %all_gains.1, f32[16,2048]{1,0:T(8,128)} %all_decay.1, f32[1,2048]{1,0:T(1,128)} %bitcast.3), custom_call_target="tpu_custom_call" | custom-call | tf_op jit(solution)/shard_map/pallas_call | solution.py:363
  181.5 2.3 %copy.8 = bf16[256,2048]{1,0:T(8,128)(2,1)} copy(bf16[256,2048]{1,0:T(8,128)(2,1)} %shard_map.64) | data formatting | bytes 2097152

commit v3 on v2

v3 whole, which is shorter than its diff:
```python
import functools

import jax
import jax.numpy as jnp
from jax import lax
from jax.experimental import pallas as pl
from jax.experimental.pallas import tpu as pltpu
from jax.sharding import PartitionSpec as P

SEGS = 8
LANES = 128


def flip(index, bits):
    out, bit = index, 1
    while bit <= bits:
        if bits & bit:
            out = out + bit - 2 * bit * ((index // bit) % 2)
        bit *= 2
    return out


def flip_traced(index, bits, count):
    out, bit = index, 1
    while bit < count:
        out = out + ((bits // bit) % 2) * (bit - 2 * bit * ((index // bit) % 2))
        bit *= 2
    return out


def piece_order(i, count):
    quarter = count // 4
    j = jnp.maximum(i - quarter, 0)
    turn = j % 3
    later = 2 * quarter + quarter * turn - 3 * quarter * (turn // 2) + j // 3
    return jnp.where(i < quarter, i, later)


def kernel(
    n_ctx, n_ch, groups,
    tokens, w_send, all_taps, all_gains, all_decay, all_skip, out,
    taps, gains, rates, skip, tok, w_recv, acc, prod, gate, state, ends, carry, sent, halo, halo_out,
    tok_ssem, tok_rsem, w_ssem, w_rsem, out_ssem, out_rsem, st_ssem, st_rsem, halo_sems, local_sems, own_sems,
):
    rows, width = tokens.shape
    wide = w_send.shape[2] // groups
    teams = n_ctx // groups
    span = groups * rows
    seg = span // SEGS
    lane_groups = wide // LANES
    ctx, ch = lax.axis_index("ctx"), lax.axis_index("ch")
    team, place = ctx // groups, ctx % groups

    hops = [("ctx", b) for b in reversed([2**i for i in range(1, groups.bit_length() - 1)])]
    hops += [("ch", b) for b in reversed([2**i for i in range(n_ch.bit_length() - 1)])]
    hops += [("ctx", 1)]
    depth = len(hops)

    def target(hop):
        axis, bit = hop
        return (flip(ctx, bit), ch) if axis == "ctx" else (ctx, flip(ch, bit))

    def slot_of(mask):
        cbits = sum(hops[i][1] for i in range(depth) if mask >> i & 1 and hops[i][0] == "ctx")
        hbits = sum(hops[i][1] for i in range(depth) if mask >> i & 1 and hops[i][0] == "ch")
        return flip(ch, hbits) * groups + flip(place, cbits)

    barrier = pltpu.get_barrier_semaphore()

    @pl.loop(1, n_ctx)
    def _(m):
        pl.semaphore_signal(barrier, inc=1, device_id=(flip_traced(ctx, m, n_ctx), ch), device_id_type=pl.DeviceIdType.MESH)

    ch_hops = [hop for hop in hops if hop[0] == "ch"]
    for hop in ch_hops:
        pl.semaphore_signal(barrier, inc=1, device_id=target(hop), device_id_type=pl.DeviceIdType.MESH)
    own_tok = pltpu.make_async_copy(tokens, tok.at[slot_of(0)], local_sems.at[0])
    own_tok.start()

    def w_columns(p, g):
        return w_send.at[:, :, pl.ds(pl.multiple_of(p * wide + g * LANES, LANES), LANES)]

    own_w = [pltpu.make_async_copy(w_columns(place, g), w_recv.at[g, 0], own_sems.at[0, g]) for g in range(lane_groups)]
    for copy in own_w:
        copy.start()
    own_lanes = pl.ds(pl.multiple_of(place * wide, LANES), wide)
    own_small = [
        pltpu.make_async_copy(all_taps.at[:, :, own_lanes], taps, local_sems.at[3]),
        pltpu.make_async_copy(all_gains.at[:, own_lanes], gains, local_sems.at[4]),
        pltpu.make_async_copy(all_decay.at[:, own_lanes], rates, local_sems.at[5]),
        pltpu.make_async_copy(all_skip.at[:, own_lanes], skip, local_sems.at[6]),
    ]
    for copy in own_small:
        copy.start()
    pl.semaphore_wait(barrier, n_ctx - 1 + len(ch_hops))

    def tok_copy(mask, i):
        src = tokens if mask == 0 else tok.at[slot_of(mask)]
        return pltpu.make_async_remote_copy(
            src_ref=src,
            dst_ref=tok.at[slot_of(mask)],
            send_sem=tok_ssem.at[mask, i],
            recv_sem=tok_rsem.at[mask | 1 << i],
            device_id=target(hops[i]),
            device_id_type=pl.DeviceIdType.MESH,
        )

    def arrived(mask):
        top = mask.bit_length() - 1
        pltpu.make_async_remote_copy(
            src_ref=tok.at[slot_of(mask)],
            dst_ref=tok.at[slot_of(mask)],
            send_sem=tok_ssem.at[0, top],
            recv_sem=tok_rsem.at[mask],
            device_id=target(hops[top]),
            device_id_type=pl.DeviceIdType.MESH,
        ).wait_recv()

    for i in range(depth):
        tok_copy(0, i).start()

    def w_copy(m, g):
        peer = flip_traced(ctx, m, n_ctx)
        return pltpu.make_async_remote_copy(
            src_ref=w_columns(peer % groups, g),
            dst_ref=w_recv.at[g, m],
            send_sem=w_ssem.at[g, m],
            recv_sem=w_rsem.at[g, m],
            device_id=(peer, ch),
            device_id_type=pl.DeviceIdType.MESH,
        )

    for g in range(lane_groups):
        @pl.loop(1, n_ctx)
        def _(i):
            w_copy(piece_order(i, n_ctx), g).start()

    acc[...] = jnp.zeros_like(acc)
    masks = sorted(range(1, 2**depth), key=lambda m: (m.bit_length() if m.bit_length() == depth else 0, bin(m).count("1"), m))
    for mask in masks:
        arrived(mask)
        for i in range(mask.bit_length(), depth):
            tok_copy(mask, i).start()
    own_tok.wait()
    for copy in own_w + own_small:
        copy.wait()
    rates[...] = rates[...] / (rows * n_ctx)

    tall = 2 if groups % 2 == 0 else 1
    header = SEGS

    modes = rates.shape[0]
    depth_rows = w_recv.shape[3]
    columns = [pl.ds(pl.multiple_of(place * wide + g * LANES, LANES), LANES) for g in range(lane_groups)]

    def project(g):
        @pl.loop(0, n_ctx)
        def _(i):
            m = piece_order(i, n_ctx)

            @pl.when(i > 0)
            def _():
                w_copy(m, g).wait_recv()

            first = flip_traced(ctx, m, n_ctx) * depth_rows
            half, column = first // width, first % width

            @pl.loop(0, groups // tall)
            def _(part):
                left = tok[pl.ds(half * groups + part * tall, tall), :, pl.ds(pl.multiple_of(column, LANES), depth_rows)]
                left = left.reshape(tall * rows, depth_rows)
                right = jnp.concatenate([w_recv[g, m, j] for j in range(3)], axis=1)
                where = pl.ds(pl.multiple_of(header + part * tall * rows, 8), tall * rows)
                acc[g, where, :] += jnp.dot(left, right, preferred_element_type=jnp.float32)

        @pl.loop(0, span // 64)
        def _(part):
            where = pl.ds(pl.multiple_of(header + part * 64, 8), 64)
            acc[g, where, :] = acc[g, where, :].astype(jnp.bfloat16).astype(jnp.float32)

    def halo_copy(g):
        return pltpu.make_async_remote_copy(
            src_ref=halo_out.at[g],
            dst_ref=halo.at[g],
            send_sem=halo_sems.at[g, 0],
            recv_sem=halo_sems.at[g, 1],
            device_id=((ctx + groups) % n_ctx, ch),
            device_id_type=pl.DeviceIdType.MESH,
        )

    def state_copy(k, g):
        return pltpu.make_async_remote_copy(
            src_ref=ends.at[g],
            dst_ref=carry.at[g, k],
            send_sem=st_ssem.at[g, k],
            recv_sem=st_rsem.at[g, k],
            device_id=((ctx + k * groups) % n_ctx, ch),
            device_id_type=pl.DeviceIdType.MESH,
        )

    def convolve(g):
        mine = slice(g * LANES, (g + 1) * LANES)
        halo_out[g] = acc[g, span : span + header, :]

        @pl.when(team < teams - 1)
        def _():
            halo_copy(g).start()

        acc[g, 0:header, :] = jnp.zeros((header, acc.shape[2]), jnp.float32)

        @pl.when(team > 0)
        def _():
            halo_copy(g).wait_recv()
            acc[g, 0:header, :] = halo[g]

        @pl.loop(0, SEGS)
        def _(s):
            base = pl.multiple_of(s * seg, 8)
            features = []
            for j in range(3):
                block = acc[g, pl.ds(base, seg + header), j * LANES : (j + 1) * LANES]
                total = taps[0, j : j + 1, mine] * block[header:]
                total += taps[1, j : j + 1, mine] * pltpu.roll(block, 1, 0)[header:]
                total += taps[2, j : j + 1, mine] * pltpu.roll(block, 2, 0)[header:]
                features.append(total)
            gate[g, pl.ds(s, seg, stride=SEGS), :] = features[0]
            prod[g, pl.ds(s, seg, stride=SEGS), :] = features[1] * features[2]

        def row(ref, m):
            return jnp.broadcast_to(ref[m : m + 1, mine], (SEGS, LANES))

        keep = [jnp.exp(-row(rates, m)) for m in range(modes)]

        def first_step(t, states):
            x = prod[g, pl.ds(pl.multiple_of(t * SEGS, SEGS), SEGS), :]
            return tuple(a * s + x for a, s in zip(keep, states))

        zeros = tuple(jnp.zeros((SEGS, LANES), jnp.float32) for _ in range(modes))
        last = lax.fori_loop(0, seg, first_step, zeros, unroll=2)
        for m in range(modes):
            state[g, m] = last[m]

        rate = rates[:, mine]
        jump = jnp.exp(-rate * float(seg))
        running = jnp.zeros_like(jump)
        for s in range(SEGS):
            ending = state[g, :, s, :]
            state[g, :, s, :] = running
            running = running * jump + ending
        ends[g] = running
        carry[g, 0] = jnp.zeros_like(jump)
        for k in range(1, teams):
            @pl.when(team + k < teams)
            def _():
                state_copy(k, g).start()
        for k in range(1, teams):
            @pl.when(team >= k)
            def _():
                state_copy(k, g).wait_recv()
                carry[g, 0] += carry[g, k] * jnp.exp(-rates[:, mine] * float((k - 1) * span))
        incoming = carry[g, 0]
        for s in range(SEGS):
            state[g, :, s, :] = state[g, :, s, :] + incoming * jnp.exp(-rate * float(s * seg))

        weight = [row(gains, m) * jnp.sqrt(2.0 * row(rates, m)) for m in range(modes)]
        direct = jnp.broadcast_to(skip[0:1, mine], (SEGS, LANES))

        def second_step(t, states):
            where = pl.ds(pl.multiple_of(t * SEGS, SEGS), SEGS)
            x = prod[g, where, :]
            states = tuple(a * s + x for a, s in zip(keep, states))
            terms = [w * s for w, s in zip(weight, states)] + [direct * x]
            while len(terms) > 1:
                terms = [a + b for a, b in zip(terms[::2], terms[1::2])] + ([terms[-1]] if len(terms) % 2 else [])
            gate[g, where, :] = gate[g, where, :] * terms[0]
            return states

        lax.fori_loop(0, seg, second_step, tuple(state[g, m] for m in range(modes)))

        @pl.loop(0, SEGS)
        def _(s):
            value = gate[g, pl.ds(s, seg, stride=SEGS), :]
            sent[g, pl.ds(pl.multiple_of(s * seg, 8), seg), :] = value.astype(sent.dtype)

    def out_rows(p, g):
        return sent.at[g, pl.ds(pl.multiple_of(p * rows, 16), rows), :]

    def out_copy(d, g):
        peer = flip_traced(place, d, groups)
        return pltpu.make_async_remote_copy(
            src_ref=out_rows(peer, g),
            dst_ref=out.at[:, columns[g]],
            send_sem=out_ssem.at[g, d],
            recv_sem=out_rsem.at[g, d],
            device_id=(team * groups + peer, ch),
            device_id_type=pl.DeviceIdType.MESH,
        )

    def out_arrival(d, g):
        peer = flip_traced(place, d, groups)
        spot = out.at[:, pl.ds(pl.multiple_of(peer * wide + g * LANES, LANES), LANES)]
        return pltpu.make_async_remote_copy(
            src_ref=spot,
            dst_ref=spot,
            send_sem=out_ssem.at[g, d],
            recv_sem=out_rsem.at[g, d],
            device_id=(team * groups + peer, ch),
            device_id_type=pl.DeviceIdType.MESH,
        )

    own_out = [pltpu.make_async_copy(out_rows(place, g), out.at[:, columns[g]], own_sems.at[1, g]) for g in range(lane_groups)]
    for g in range(lane_groups):
        project(g)
        convolve(g)

        @pl.loop(1, groups)
        def _(d):
            out_copy(groups - d, g).start()

        own_out[g].start()

    for i in range(depth):
        tok_copy(0, i).wait_send()
    for mask in masks:
        for i in range(mask.bit_length(), depth):
            tok_copy(mask, i).wait_send()

    for g in range(lane_groups):
        @pl.loop(1, n_ctx)
        def _(m):
            w_copy(m, g).wait_send()

        @pl.when(team < teams - 1)
        def _():
            halo_copy(g).wait_send()

        for k in range(1, teams):
            @pl.when(team + k < teams)
            def _():
                state_copy(k, g).wait_send()

        @pl.loop(1, groups)
        def _(d):
            out_arrival(d, g).wait_recv()
            out_copy(d, g).wait_send()

        own_out[g].wait()


def body(n_ctx, n_ch, tokens, w_in, taps, modes_gain, decay, skip):
    rows, width = tokens.shape
    e_rows, _, channels = w_in.shape
    modes = decay.shape[0]
    groups = min(n_ctx // 2, channels // LANES)
    teams = n_ctx // groups
    wide = channels // groups
    span = groups * rows
    parts = wide // LANES
    depth = (groups * n_ch).bit_length() - 1
    w_send = w_in.transpose(1, 0, 2)
    hbm = pl.BlockSpec(memory_space=pl.ANY)
    dma = pltpu.SemaphoreType.DMA
    f32 = jnp.float32
    return pl.pallas_call(
        functools.partial(kernel, n_ctx, n_ch, groups),
        out_shape=jax.ShapeDtypeStruct((rows, channels), jnp.bfloat16),
        in_specs=[hbm] * 6,
        out_specs=hbm,
        scratch_shapes=[
            pltpu.VMEM((3, 3, wide), f32),
            pltpu.VMEM((modes, wide), f32),
            pltpu.VMEM((modes, wide), f32),
            pltpu.VMEM((1, wide), f32),
            pltpu.VMEM((n_ch * groups, rows, width), tokens.dtype),
            pltpu.VMEM((parts, n_ctx, 3, e_rows, LANES), w_in.dtype),
            pltpu.VMEM((parts, SEGS + span, 3 * LANES), f32),
            pltpu.VMEM((parts, span, LANES), f32),
            pltpu.VMEM((parts, span, LANES), f32),
            pltpu.VMEM((parts, modes, SEGS, LANES), f32),
            pltpu.VMEM((parts, modes, LANES), f32),
            pltpu.VMEM((parts, teams, modes, LANES), f32),
            pltpu.VMEM((parts, span, LANES), jnp.bfloat16),
            pltpu.VMEM((parts, SEGS, 3 * LANES), f32),
            pltpu.VMEM((parts, SEGS, 3 * LANES), f32),
            dma((2**depth, depth)),
            dma((2**depth,)),
            dma((parts, n_ctx)),
            dma((parts, n_ctx)),
            dma((parts, groups)),
            dma((parts, groups)),
            dma((parts, teams)),
            dma((parts, teams)),
            dma((parts, 2)),
            dma((7,)),
            dma((2, parts)),
        ],
        compiler_params=pltpu.CompilerParams(
            collective_id=0, has_side_effects=True, vmem_limit_bytes=60 * 1024 * 1024
        ),
    )(tokens, w_send, taps, modes_gain, decay, skip[None])


def solution(mesh):
    in_specs = (
        P("ctx", "ch"),
        P("ctx", None, "ch"),
        P(None, None, "ch"),
        P(None, "ch"),
        P(None, "ch"),
        P("ch"),
    )
    step = functools.partial(body, mesh.shape["ctx"], mesh.shape["ch"])
    return jax.shard_map(step, mesh=mesh, in_specs=in_specs, out_specs=P("ctx", "ch"), check_vma=False)
```

time: 184 us -> 193 us (1.049)
  Pallas kernels: 181 us -> 189 us
    pallas_call x1, Pallas kernels: 181 us -> 189 us  [body(): pl.pallas_call(functools.partial(kernel, n_ctx, n_ch, groups), out_shape=...]
where the time goes in v3:
time: 193 us; the launch traced here: 192 us
  Pallas kernels  189 us (98%)
  local copies, waits for them, and re-layouts  2.3 us (1%)
    pallas_call x1, Pallas kernels, body(): pl.pallas_call(functools.partial(kernel, n_ctx, n_ch, groups), out_shape=...  189 us

profile of v3, /device:TPU:16, one launch (start us, length us, event | category | flops | bytes accessed | tf_op | source)
XLA Modules:
  0.0 191.7 jit_solution(12801650327273558783)
XLA Ops:
  0.0 189.4 %shard_map.64 = bf16[256,2048]{1,0:T(8,128)(2,1)} custom-call(bf16[256,2048]{1,0:T(8,128)(2,1)} %tokens.1, bf16[3,256,2048]{2,1,0:T(8,128)(2,1)} %bitcast.2, f32[3,3,2048]{2,1,0:T(4,128)} %all_taps.1, f32[16,2048]{1,0:T(8,128)} %all_gains.1, f32[16,2048]{1,0:T(8,128)} %all_decay.1, f32[1,2048]{1,0:T(1,128)} %bitcast.3), custom_call_target="tpu_custom_call" | custom-call | tf_op jit(solution)/shard_map/pallas_call | solution.py:364
  189.4 2.3 %copy.8 = bf16[256,2048]{1,0:T(8,128)(2,1)} copy(bf16[256,2048]{1,0:T(8,128)(2,1)} %shard_map.64) | data formatting | bytes 2097152

commit v4 on v3

--- a/solution.py
+++ b/solution.py
@@ -32,7 +32,7 @@
     quarter = count // 4
     j = jnp.maximum(i - quarter, 0)
     turn = j % 3
-    later = 2 * quarter + quarter * turn - 3 * quarter * (turn // 2) + j // 3
+    later = quarter + quarter * turn + j // 3
     return jnp.where(i < quarter, i, later)
 
 
@@ -133,7 +133,7 @@
     for g in range(lane_groups):
         @pl.loop(1, n_ctx)
         def _(i):
-            w_copy(piece_order(i, n_ctx), g).start()
+            w_copy(2 * piece_order(i // 2, n_ctx // 2) + i % 2, g).start()
 
     acc[...] = jnp.zeros_like(acc)
     masks = sorted(range(1, 2**depth), key=lambda m: (m.bit_length() if m.bit_length() == depth else 0, bin(m).count("1"), m))
@@ -146,7 +146,7 @@
         copy.wait()
     rates[...] = rates[...] / (rows * n_ctx)
 
-    tall = 2 if groups % 2 == 0 else 1
+    tall = 4 if groups % 4 == 0 else 1
     header = SEGS
 
     modes = rates.shape[0]
@@ -154,22 +154,27 @@
     columns = [pl.ds(pl.multiple_of(place * wide + g * LANES, LANES), LANES) for g in range(lane_groups)]
 
     def project(g):
-        @pl.loop(0, n_ctx)
+        @pl.loop(0, n_ctx // 2)
         def _(i):
-            m = piece_order(i, n_ctx)
+            m = 2 * piece_order(i, n_ctx // 2)
+            odd = ctx % 2
 
             @pl.when(i > 0)
             def _():
                 w_copy(m, g).wait_recv()
 
-            first = flip_traced(ctx, m, n_ctx) * depth_rows
+            w_copy(m + 1, g).wait_recv()
+            first = flip_traced(ctx - odd, m, n_ctx) * depth_rows
             half, column = first // width, first % width
 
             @pl.loop(0, groups // tall)
             def _(part):
-                left = tok[pl.ds(half * groups + part * tall, tall), :, pl.ds(pl.multiple_of(column, LANES), depth_rows)]
-                left = left.reshape(tall * rows, depth_rows)
-                right = jnp.concatenate([w_recv[g, m, j] for j in range(3)], axis=1)
+                left = tok[pl.ds(half * groups + part * tall, tall), :, pl.ds(pl.multiple_of(column, LANES), 2 * depth_rows)]
+                left = left.reshape(tall * rows, 2 * depth_rows)
+                pair = (m + odd, m + 1 - odd)
+                right = jnp.concatenate(
+                    [jnp.concatenate([w_recv[g, p, j] for p in pair], axis=0) for j in range(3)], axis=1
+                )
                 where = pl.ds(pl.multiple_of(header + part * tall * rows, 8), tall * rows)
                 acc[g, where, :] += jnp.dot(left, right, preferred_element_type=jnp.float32)
 

time: 193 us -> 179 us (0.927)
  Pallas kernels: 189 us -> 176 us
    pallas_call x1, Pallas kernels: 189 us -> 176 us  [body(): pl.pallas_call(functools.partial(kernel, n_ctx, n_ch, groups), out_shape=...]
where the time goes in v4:
time: 179 us
  Pallas kernels  176 us (98%)
  local copies, waits for them, and re-layouts  2.3 us (1%)
    pallas_call x1, Pallas kernels, body(): pl.pallas_call(functools.partial(kernel, n_ctx, n_ch, groups), out_shape=...  176 us

profile of v4, /device:TPU:16, one launch (start us, length us, event | category | flops | bytes accessed | tf_op | source)
XLA Modules:
  0.0 178.5 jit_solution(14882165505608622960)
XLA Ops:
  0.0 176.2 %shard_map.64 = bf16[256,2048]{1,0:T(8,128)(2,1)} custom-call(bf16[256,2048]{1,0:T(8,128)(2,1)} %tokens.1, bf16[3,256,2048]{2,1,0:T(8,128)(2,1)} %bitcast.2, f32[3,3,2048]{2,1,0:T(4,128)} %all_taps.1, f32[16,2048]{1,0:T(8,128)} %all_gains.1, f32[16,2048]{1,0:T(8,128)} %all_decay.1, f32[1,2048]{1,0:T(1,128)} %bitcast.3), custom_call_target="tpu_custom_call" | custom-call | tf_op jit(solution)/shard_map/pallas_call | solution.py:369
  176.2 2.3 %copy.8 = bf16[256,2048]{1,0:T(8,128)(2,1)} copy(bf16[256,2048]{1,0:T(8,128)(2,1)} %shard_map.64) | data formatting | bytes 2097152

commit v5 on v4

--- a/solution.py
+++ b/solution.py
@@ -146,7 +146,7 @@
         copy.wait()
     rates[...] = rates[...] / (rows * n_ctx)
 
-    tall = 4 if groups % 4 == 0 else 1
+    tall = groups
     header = SEGS
 
     modes = rates.shape[0]

time: 179 us -> 177 us (0.989)
  no operation moved by 1% of the time
where the time goes in v5:
time: 177 us
  Pallas kernels  175 us (99%)
  local copies, waits for them, and re-layouts  2.3 us (1%)
    pallas_call x1, Pallas kernels, body(): pl.pallas_call(functools.partial(kernel, n_ctx, n_ch, groups), out_shape=...  175 us

profile of v5, /device:TPU:16, one launch (start us, length us, event | category | flops | bytes accessed | tf_op | source)
XLA Modules:
  0.0 176.9 jit_solution(1595010294927140119)
XLA Ops:
  0.0 174.6 %shard_map.64 = bf16[256,2048]{1,0:T(8,128)(2,1)} custom-call(bf16[256,2048]{1,0:T(8,128)(2,1)} %tokens.1, bf16[3,256,2048]{2,1,0:T(8,128)(2,1)} %bitcast.2, f32[3,3,2048]{2,1,0:T(4,128)} %all_taps.1, f32[16,2048]{1,0:T(8,128)} %all_gains.1, f32[16,2048]{1,0:T(8,128)} %all_decay.1, f32[1,2048]{1,0:T(1,128)} %bitcast.3), custom_call_target="tpu_custom_call" | custom-call | tf_op jit(solution)/shard_map/pallas_call | solution.py:369
  174.6 2.3 %copy.8 = bf16[256,2048]{1,0:T(8,128)(2,1)} copy(bf16[256,2048]{1,0:T(8,128)(2,1)} %shard_map.64) | data formatting | bytes 2097152
